TPU v7x, 32 devices: a whole 2x2x4 slice. The times are simulated.
32 devices in a mesh: wide: 8 (over z, y), narrow: 4 (over x, core).
Axes of the slice: x: 2, y: 2, z: 4, core: 2. Of those that a mesh axis runs over, the one named last changes fastest.
Arguments:
- panel: float32 [16384, 128], P(('wide', 'narrow')), may hold values from -40 to 40
- trailing: float32 [16384, 256], P(('wide', 'narrow')), may hold values from -40 to 40
Outputs:
- q_factor: float32 [16384, 128], P(('wide', 'narrow'))
- r_factor: float32 [128, 128], replicated
- projection: float32 [128, 256], replicated
- updated: float32 [16384, 256], P(('wide', 'narrow'))
All inputs are finite; a program needn't handle non-finite values.
Results may differ from a plain program's by a relative error of at most 0.00045.
Values sent between devices are 32-bit elements; how exact they have to be, the bound alone decides.
No kernel may reach another device: no remote copies, remote signals or barrier semaphores. Data moves between devices by JAX's collectives and lax.ppermute only.
A program may use at most 64 MiB of HBM per device.

v0:
```python
import jax
import jax.numpy as jnp
from jax import lax
from jax.sharding import PartitionSpec as P


def upper_factor(gram_matrix):
    order = gram_matrix.shape[0]
    columns = jnp.arange(order, dtype=jnp.int32)

    def column_step(index, state):
        work, factor = state
        where = jnp.asarray(index).astype(jnp.int32)
        pivot_row = lax.dynamic_index_in_dim(work, where, 0, keepdims=False)
        pivot = lax.dynamic_index_in_dim(pivot_row, where, 0, keepdims=False)
        new_row = jnp.where(
            columns >= where, pivot_row / jnp.sqrt(pivot), jnp.zeros_like(pivot_row)
        )
        work = work - new_row[:, None] * new_row[None, :]
        factor = lax.dynamic_update_slice_in_dim(factor, new_row[None, :], where, 0)
        return (work, factor)

    start = (gram_matrix, jnp.zeros_like(gram_matrix))
    return lax.fori_loop(0, order, column_step, start)[1]


def inverse_upper(upper_part):
    order = upper_part.shape[0]
    identity = jnp.eye(order, dtype=upper_part.dtype)

    def row_step(count, inverse):
        where = (order - 1 - jnp.asarray(count)).astype(jnp.int32)
        upper_row = lax.dynamic_index_in_dim(upper_part, where, 0, keepdims=False)
        unit_row = lax.dynamic_index_in_dim(identity, where, 0, keepdims=False)
        pivot = lax.dynamic_index_in_dim(upper_row, where, 0, keepdims=False)
        partial_value = jnp.dot(upper_row, inverse, precision=lax.Precision.HIGHEST)
        new_row = (unit_row - partial_value) / pivot
        return lax.dynamic_update_slice_in_dim(inverse, new_row[None, :], where, 0)

    return lax.fori_loop(0, order, row_step, jnp.zeros_like(upper_part))


def product(left, right):
    return jnp.dot(left, right, precision=lax.Precision.HIGHEST, preferred_element_type=jnp.float32)


def on_device(panel, trailing):
    row_total = float(panel.shape[0] * lax.axis_size("wide") * lax.axis_size("narrow"))
    gram_local = product(panel.T, panel) / row_total
    cross_local = product(panel.T, trailing) / row_total
    gram_first, cross_terms = lax.psum((gram_local, cross_local), ("wide", "narrow"))
    first_factor = upper_factor(gram_first)
    basis_rows = product(panel, inverse_upper(first_factor))
    gram_second = lax.psum(product(basis_rows.T, basis_rows) / row_total, ("wide", "narrow"))
    second_factor = upper_factor(gram_second)
    q_factor = product(basis_rows, inverse_upper(second_factor))
    r_factor = product(second_factor, first_factor)
    projection = product(inverse_upper(r_factor).T, cross_terms)
    updated = trailing - product(q_factor, projection)
    return (q_factor, r_factor, projection, updated)


def solution(mesh):
    in_specs = (P(("wide", "narrow"), None), P(("wide", "narrow"), None))
    out_specs = (P(("wide", "narrow"), None), P(), P(), P(("wide", "narrow"), None))
    return jax.shard_map(
        on_device, mesh=mesh, in_specs=in_specs, out_specs=out_specs, check_vma=False
    )
```

profile of v0, /device:TPU:8, one launch (start us, length us, event | category | flops | bytes accessed | tf_op | source)
XLA Modules:
  0.0 1208.6 jit_solution(7260193359423582820)
XLA Ops:
  7.2 0.9 copy-done
  8.1 1.2 convolution_multiply_fusion.2
  9.4 1.3 convolution_multiply_fusion
  10.7 125.4 %all-reduce.4.cloned.1.call-done = f32[128,128]{1,0:T(8,128)} async-done(((f32[128,128]{1,0:T(8,128)}), f32[128,128]{1,0:T(8,128)}) %all-reduce.4.cloned.1.call-update) | async-done | bytes 65552 | tf_op jit(solution)/shard_map/psum | solution.py:51
  136.1 0.8 copy-done.3
  137.0 188.3 %while.89 = (s32[]{:T(128)}, f32[128,128]{1,0:T(8,128)S(1)}, f32[128,128]{1,0:T(8,128)S(1)}, s32[]{:T(128)}, s32[]{:T(128)}, /*index=5*/s32[]{:T(128)}) while((s32[]{:T(128)}, f32[128,128]{1,0:T(8,128)S(1)}, f32[128,128]{1,0:T(8,128)S(1)}, s32[]{:T(128)}, s32[]{:T(128)}, /*index=5*/s32[]{:T(128)}) %tuple.212), condition=%wide.region_2.3_spmd.clone, body=%wide.region_1.0_spmd.clone.sunk | while | flops 33667 | bytes 138357 | solution.py:24
  325.2 185.2 %while.86 = (s32[]{:T(128)}, f32[128,128]{1,0:T(8,128)S(1)}, f32[128,128]{1,0:T(8,128)S(1)}, f32[128,128]{1,0:T(8,128)S(1)}, s32[]{:T(128)}, /*index=5*/s32[]{:T(128)}, s32[]{:T(128)}, s32[]{:T(128)}) while((s32[]{:T(128)}, f32[128,128]{1,0:T(8,128)S(1)}, f32[128,128]{1,0:T(8,128)S(1)}, f32[128,128]{1,0:T(8,128)S(1)}, s32[]{:T(128)}, ...), condition=%wide.region_4.5_spmd, body=%wide.region_3.4_spmd.sunk | while | flops 196871 | bytes 69287 | solution.py:40
  334.5 0.8 fusion.61
  336.0 0.8 fusion.61
  337.4 0.8 fusion.61
  338.9 0.8 fusion.61
  347.6 0.8 fusion.61
  349.0 0.8 fusion.61
  350.5 0.8 fusion.61
  351.9 0.8 fusion.61
  362.0 0.8 fusion.61
  363.5 0.8 fusion.61
  364.9 0.8 fusion.61
  366.4 0.8 fusion.61
  375.1 0.8 fusion.61
  376.5 0.8 fusion.61
  377.9 0.8 fusion.61
  379.4 0.8 fusion.61
  389.5 0.8 fusion.61
  391.0 0.8 fusion.61
  392.4 0.8 fusion.61
  393.9 0.8 fusion.61
  402.5 0.8 fusion.61
  404.0 0.8 fusion.61
  405.4 0.8 fusion.61
  406.9 0.8 fusion.61
  417.0 0.8 fusion.61
  418.5 0.8 fusion.61
  419.9 0.8 fusion.61
  421.4 0.8 fusion.61
  430.0 0.8 fusion.61
  431.5 0.8 fusion.61
  432.9 0.8 fusion.61
  434.4 0.8 fusion.61
  444.5 0.8 fusion.61
  445.9 0.8 fusion.61
  510.9 1.0 convolution_multiply_fusion.1
  511.9 126.9 %all-reduce.6.cloned.1.call-done = (f32[128,128]{1,0:T(8,128)}, f32[128,256]{1,0:T(8,128)}) async-done(((f32[128,128]{1,0:T(8,128)}, f32[128,256]{1,0:T(8,128)}), (f32[128,128]{1,0:T(8,128)}, f32[128,256]{1,0:T(8,128)})) %all-reduce.6.cloned.1.call-update) | async-done | bytes 196624 | tf_op jit(solution)/shard_map/psum | solution.py:54
  638.8 0.8 copy-done.2
  639.6 188.3 %while.90 = (s32[]{:T(128)}, f32[128,128]{1,0:T(8,128)S(1)}, f32[128,128]{1,0:T(8,128)S(1)}, s32[]{:T(128)}, s32[]{:T(128)}, /*index=5*/s32[]{:T(128)}) while((s32[]{:T(128)}, f32[128,128]{1,0:T(8,128)S(1)}, f32[128,128]{1,0:T(8,128)S(1)}, s32[]{:T(128)}, s32[]{:T(128)}, /*index=5*/s32[]{:T(128)}) %tuple.211), condition=%wide.region_7.8_spmd.clone, body=%wide.region_6.7_spmd.clone.sunk | while | flops 33667 | bytes 138357 | solution.py:24
  828.1 185.2 %while.88 = (s32[]{:T(128)}, f32[128,128]{1,0:T(8,128)S(1)}, f32[128,128]{1,0:T(8,128)S(1)}, f32[128,128]{1,0:T(8,128)S(1)}, s32[]{:T(128)}, /*index=5*/s32[]{:T(128)}, s32[]{:T(128)}, s32[]{:T(128)}) while((s32[]{:T(128)}, f32[128,128]{1,0:T(8,128)S(1)}, f32[128,128]{1,0:T(8,128)S(1)}, f32[128,128]{1,0:T(8,128)S(1)}, s32[]{:T(128)}, ...), condition=%wide.region_11.12_spmd, body=%wide.region_10.11_spmd.sunk | while | flops 196871 | bytes 69287 | solution.py:40
  1014.0 185.2 %while.87 = (s32[]{:T(128)}, f32[128,128]{1,0:T(8,128)S(1)}, f32[128,128]{1,0:T(8,128)S(1)}, f32[128,128]{1,0:T(8,128)S(1)}, s32[]{:T(128)}, /*index=5*/s32[]{:T(128)}, s32[]{:T(128)}, s32[]{:T(128)}) while((s32[]{:T(128)}, f32[128,128]{1,0:T(8,128)S(1)}, f32[128,128]{1,0:T(8,128)S(1)}, f32[128,128]{1,0:T(8,128)S(1)}, s32[]{:T(128)}, ...), condition=%wide.region_9.10_spmd, body=%wide.region_8.9_spmd.sunk | while | flops 196871 | bytes 69287 | solution.py:40
  1200.4 1.4 convolution_subtract_fusion
  (2681 shorter events, 706.1 us)
Async XLA Ops:
  7.2 1.0 copy-start
  7.2 2.2 copy-start.1
  7.2 128.9 %all-reduce.4.cloned.1.call-start = ((), (), s32[]{:S(2)}) async-start(), calls=%async_computation | async-start | bytes 131072 | tf_op jit(solution)/shard_map/psum | solution.py:51
  9.4 629.4 %all-reduce.6.cloned.1.call-start = ((), (), s32[]{:S(2)}) async-start(), calls=%async_computation.1 | async-start | bytes 393216 | tf_op jit(solution)/shard_map/psum | solution.py:54
  136.1 0.8 copy-start.3
  638.8 0.8 copy-start.2
  1013.3 0.6 copy-start.7
  1199.1 0.9 copy-start.6
  1199.7 2.0 copy-start.4
  1200.4 1.4 copy-start.5
Sparse Core Ops, SparseCore 0:
  14.2 121.9 all-reduce.3
  512.0 126.6 all-reduce.5
where the time goes:
time: 1220 us; the launch traced here: 1210 us
  local copies, waits for them, and re-layouts  401 us (33%)
  matrix products  313 us (26%)
  waiting for transfers between devices  252 us (21%)
  loops' own time  202 us (17%)
  other arithmetic  26.6 us (2%)
  between operations  14.2 us (1%)
    dot_general x384, matrix products, row_step(): partial_value = jnp.dot(upper_row, inverse, precision=lax.Precision.HIGHEST)  306 us
    dynamic_slice x384, local copies, waits for them, and re-layouts, row_step(): pivot = lax.dynamic_index_in_dim(upper_row, where, 0, keepdims=False)  226 us
    another operation x2, loops' own time, upper_factor(): return lax.fori_loop(0, order, column_step, start)[1]  190 us
    dynamic_slice x256, local copies, waits for them, and re-layouts, column_step(): pivot = lax.dynamic_index_in_dim(pivot_row, where, 0, keepdims=False)  151 us
    psum x1, waiting for transfers between devices, on_device(): lax.psum(product(basis_rows.T, basis_rows) / row_total, ('wide', 'narrow'))  127 us
    psum x1, waiting for transfers between devices, on_device(): lax.psum((gram_local, cross_local), ('wide', 'narrow'))  125 us
  transfers between devices with their start and end apart: 2, of which 2 were waited for; matrix products, arithmetic and copies ran while one was open for 0% of the time, Pallas kernels for 0%

commit v1 on v0

--- a/solution.py
+++ b/solution.py
@@ -51,7 +51,9 @@
     gram_first, cross_terms = lax.psum((gram_local, cross_local), ("wide", "narrow"))
     first_factor = upper_factor(gram_first)
     basis_rows = product(panel, inverse_upper(first_factor))
-    gram_second = lax.psum(product(basis_rows.T, basis_rows) / row_total, ("wide", "narrow"))
+    x = product(basis_rows.T, basis_rows) / row_total
+    pieces = lax.all_gather(x, ("wide", "narrow"))
+    gram_second = jnp.sum(pieces, axis=0)
     second_factor = upper_factor(gram_second)
     q_factor = product(basis_rows, inverse_upper(second_factor))
     r_factor = product(second_factor, first_factor)

time: 1220 us -> 1520 us (1.25)
  other arithmetic: 26.6 us -> 302 us
  local copies, waits for them, and re-layouts: 401 us -> 484 us
  waiting for transfers between devices: 252 us -> 185 us
    sub x256, other arithmetic: 21 us -> 208 us  [column_step(): work = work - new_row[:, None] * new_row[None, :]]
    psum x1 -> x0, waiting for transfers between devices: 127 us -> none  [on_device(): lax.psum(product(basis_rows.T, basis_rows) / row_total, ('wide', 'narrow'))]
    select_n x512, other arithmetic: 4.58 us -> 91.5 us  [column_step(): jnp.where(columns >= where, pivot_row / jnp.sqrt(pivot), jnp.zeros_like(p...]
    dynamic_slice x256, local copies, waits for them, and re-layouts: 151 us -> 237 us  [column_step(): pivot = lax.dynamic_index_in_dim(pivot_row, where, 0, keepdims=False)]
    all_gather x0 -> x1, waiting for transfers between devices: none -> 54.5 us  [on_device(): pieces = lax.all_gather(x, ('wide', 'narrow'))]
where the time goes in v1:
time: 1520 us; the launch traced here: 1500 us
  local copies, waits for them, and re-layouts  484 us (32%)
  matrix products  314 us (21%)
  other arithmetic  302 us (20%)
  loops' own time  197 us (13%)
  waiting for transfers between devices  185 us (12%)
    dot_general x384, matrix products, row_step(): partial_value = jnp.dot(upper_row, inverse, precision=lax.Precision.HIGHEST)  306 us
    dynamic_slice x256, local copies, waits for them, and re-layouts, column_step(): pivot = lax.dynamic_index_in_dim(pivot_row, where, 0, keepdims=False)  237 us
    dynamic_slice x384, local copies, waits for them, and re-layouts, row_step(): pivot = lax.dynamic_index_in_dim(upper_row, where, 0, keepdims=False)  226 us
    sub x256, other arithmetic, column_step(): work = work - new_row[:, None] * new_row[None, :]  208 us
    another operation x2, loops' own time, upper_factor(): return lax.fori_loop(0, order, column_step, start)[1]  185 us
    psum x1, waiting for transfers between devices, on_device(): lax.psum((gram_local, cross_local), ('wide', 'narrow'))  130 us
    select_n x512, other arithmetic, column_step(): jnp.where(columns >= where, pivot_row / jnp.sqrt(pivot), jnp.zeros_like(p...  91.5 us
    all_gather x1, waiting for transfers between devices, on_device(): pieces = lax.all_gather(x, ('wide', 'narrow'))  54.5 us
  transfers between devices with their start and end apart: 2, of which 2 were waited for; matrix products, arithmetic and copies ran while one was open for 0% of the time, Pallas kernels for 0%

profile of v1, /device:TPU:8, one launch (start us, length us, event | category | flops | bytes accessed | tf_op | source)
XLA Modules:
  0.0 1495.1 jit_solution(8024177847361000524)
XLA Ops:
  9.3 2.3 convolution_multiply_fusion
  11.7 130.5 %all-reduce.3.cloned.1.call-done = (f32[128,128]{1,0:T(8,128)}, f32[128,256]{1,0:T(8,128)}) async-done(((f32[128,128]{1,0:T(8,128)}, f32[128,256]{1,0:T(8,128)}), (f32[128,128]{1,0:T(8,128)}, f32[128,256]{1,0:T(8,128)})) %all-reduce.3.cloned.1.call-update) | async-done | bytes 196624 | tf_op jit(solution)/shard_map/psum | solution.py:51
  142.2 542.0 %while.89 = (s32[]{:T(128)}, f32[128,128]{1,0:T(8,128)}, f32[128,128]{1,0:T(8,128)S(1)}, s32[]{:T(128)}, s32[]{:T(128)}, /*index=5*/s32[]{:T(128)}) while((s32[]{:T(128)}, f32[128,128]{1,0:T(8,128)}, f32[128,128]{1,0:T(8,128)S(1)}, s32[]{:T(128)}, s32[]{:T(128)}, /*index=5*/s32[]{:T(128)}) %tuple.191), condition=%wide.region_2.3_spmd.clone, body=%wide.region_1.0_spmd.clone.sunk | while | flops 33667 | bytes 138357 | solution.py:24
  144.9 1.5 multiply_subtract_fusion.4
  149.1 1.5 multiply_subtract_fusion.4
  153.3 1.5 multiply_subtract_fusion.4
  157.6 1.5 multiply_subtract_fusion.4
  161.8 1.5 multiply_subtract_fusion.4
  166.0 1.5 multiply_subtract_fusion.4
  170.2 1.5 multiply_subtract_fusion.4
  174.5 1.5 multiply_subtract_fusion.4
  178.7 1.5 multiply_subtract_fusion.4
  182.9 1.5 multiply_subtract_fusion.4
  187.2 1.5 multiply_subtract_fusion.4
  191.4 1.5 multiply_subtract_fusion.4
  195.6 1.5 multiply_subtract_fusion.4
  199.8 1.5 multiply_subtract_fusion.4
  204.0 1.5 multiply_subtract_fusion.4
  208.3 1.5 multiply_subtract_fusion.4
  212.5 1.5 multiply_subtract_fusion.4
  229.5 1.5 multiply_subtract_fusion.4
  242.2 1.5 multiply_subtract_fusion.4
  263.4 1.5 multiply_subtract_fusion.4
  276.1 1.5 multiply_subtract_fusion.4
  293.1 1.5 multiply_subtract_fusion.4
  297.4 1.5 multiply_subtract_fusion.4
  314.3 1.5 multiply_subtract_fusion.4
  331.3 1.5 multiply_subtract_fusion.4
  386.2 1.5 multiply_subtract_fusion.4
  407.4 1.5 multiply_subtract_fusion.4
  428.6 1.5 multiply_subtract_fusion.4
  432.8 1.5 multiply_subtract_fusion.4
  437.0 1.5 multiply_subtract_fusion.4
  454.0 1.5 multiply_subtract_fusion.4
  475.2 1.5 multiply_subtract_fusion.4
  492.1 1.5 multiply_subtract_fusion.4
  496.4 1.5 multiply_subtract_fusion.4
  513.3 1.5 multiply_subtract_fusion.4
  538.6 1.5 multiply_subtract_fusion.4
  581.0 1.5 multiply_subtract_fusion.4
  593.6 1.5 multiply_subtract_fusion.4
  610.5 1.5 multiply_subtract_fusion.4
  684.2 185.2 %while.86 = (s32[]{:T(128)}, f32[128,128]{1,0:T(8,128)S(1)}, f32[128,128]{1,0:T(8,128)S(1)}, f32[128,128]{1,0:T(8,128)S(1)}, s32[]{:T(128)}, /*index=5*/s32[]{:T(128)}, s32[]{:T(128)}, s32[]{:T(128)}) while((s32[]{:T(128)}, f32[128,128]{1,0:T(8,128)S(1)}, f32[128,128]{1,0:T(8,128)S(1)}, f32[128,128]{1,0:T(8,128)S(1)}, s32[]{:T(128)}, ...), condition=%wide.region_4.5_spmd, body=%wide.region_3.4_spmd.sunk | while | flops 196871 | bytes 69287 | solution.py:40
  870.8 54.5 %all-gather.3.cloned.1.call-done = f32[4096,128]{1,0:T(8,128)} async-done(((f32[128,128]{1,0:T(8,128)}), f32[4096,128]{1,0:T(8,128)}) %all-gather.3.cloned.1.call-update) | async-done | bytes 2097168 | tf_op jit(solution)/shard_map/all_gather | solution.py:55
  925.3 1.7 reduce_sum.9
  927.1 188.3 %while.90 = (s32[]{:T(128)}, f32[128,128]{1,0:T(8,128)S(1)}, f32[128,128]{1,0:T(8,128)S(1)}, s32[]{:T(128)}, s32[]{:T(128)}, /*index=5*/s32[]{:T(128)}) while((s32[]{:T(128)}, f32[128,128]{1,0:T(8,128)S(1)}, f32[128,128]{1,0:T(8,128)S(1)}, s32[]{:T(128)}, s32[]{:T(128)}, /*index=5*/s32[]{:T(128)}) %tuple.197), condition=%wide.region_7.8_spmd.clone, body=%wide.region_6.7_spmd.clone.sunk | while | flops 33667 | bytes 138357 | solution.py:24
  1115.6 185.2 %while.87 = (s32[]{:T(128)}, f32[128,128]{1,0:T(8,128)S(1)}, f32[128,128]{1,0:T(8,128)S(1)}, f32[128,128]{1,0:T(8,128)S(1)}, s32[]{:T(128)}, /*index=5*/s32[]{:T(128)}, s32[]{:T(128)}, s32[]{:T(128)}) while((s32[]{:T(128)}, f32[128,128]{1,0:T(8,128)S(1)}, f32[128,128]{1,0:T(8,128)S(1)}, f32[128,128]{1,0:T(8,128)S(1)}, s32[]{:T(128)}, ...), condition=%wide.region_9.10_spmd, body=%wide.region_8.9_spmd.sunk | while | flops 196871 | bytes 69287 | solution.py:40
  1301.4 185.1 %while.88 = (s32[]{:T(128)}, f32[128,128]{1,0:T(8,128)S(1)}, f32[128,128]{1,0:T(8,128)S(1)}, f32[128,128]{1,0:T(8,128)S(1)}, s32[]{:T(128)}, /*index=5*/s32[]{:T(128)}, s32[]{:T(128)}, s32[]{:T(128)}) while((s32[]{:T(128)}, f32[128,128]{1,0:T(8,128)S(1)}, f32[128,128]{1,0:T(8,128)S(1)}, f32[128,128]{1,0:T(8,128)S(1)}, s32[]{:T(128)}, ...), condition=%wide.region_11.12_spmd, body=%wide.region_10.11_spmd.sunk | while | flops 196871 | bytes 69287 | solution.py:40
  (2678 shorter events, 1035.3 us)
Async XLA Ops:
  7.2 1.0 copy-start
  7.2 135.0 %all-reduce.3.cloned.1.call-start = ((), (), s32[]{:S(2)}) async-start(), calls=%async_computation.1 | async-start | bytes 393216 | tf_op jit(solution)/shard_map/psum | solution.py:51
  11.7 913.6 %all-gather.3.cloned.1.call-start = ((), (), s32[]{:S(2)}) async-start(), calls=%async_computation | async-start | bytes 2162688 | tf_op jit(solution)/shard_map/all_gather | solution.py:55
  925.3 561.3 %copy-start.4 = (f32[128,256]{1,0:T(8,128)S(1)}, f32[128,256]{1,0:T(8,128)}, u32[]{:S(2)}) copy-start(f32[128,256]{1,0:T(8,128)} %get-tuple-element.691) | copy-start | bytes 393220
  927.0 559.8 %copy-start.1 = (f32[512,256]{1,0:T(8,128)S(1)}, f32[512,256]{1,0:T(8,128)}, u32[]{:S(2)}) copy-start(f32[512,256]{1,0:T(8,128)} %param.13) | copy-start | bytes 1572868
  1301.4 186.9 %copy-start.2 = (f32[512,128]{1,0:T(8,128)}, f32[512,128]{1,0:T(8,128)S(1)}, u32[]{:S(2)}) copy-start(f32[512,128]{1,0:T(8,128)S(1)} %fusion.24) | copy-start | bytes 786436
  1486.6 1.7 copy-start.5
  1486.9 1.4 copy-start.3
Sparse Core Ops, SparseCore 0:
  14.2 127.9 all-reduce.2
  871.0 54.2 all-gather.2
